TPU v7x, 512 devices: a whole 4x8x8 slice. The times are simulated.
512 devices in a mesh: batch: 32 (over z, y_hi), weight: 16 (over x, y_lo, core).
Axes of the slice: x: 4, y: 8 (y_hi: 4, y_lo: 2; y = y_hi * 2 + y_lo), z: 8, core: 2. Of those that a mesh axis runs over, the one named last changes fastest.
Arguments:
- tokens: bfloat16 [16384, 8192], P(('batch', 'weight')), may hold values from -6 to 6
- segment_ids: int32 [16384], P('batch'), may hold values from 0 to 511, never falling along the last dimension, each value on 1 to 64 neighbouring positions
- norm_gain: float32 [8192], replicated, may hold values from 0.1 to 1.9
- query_weight: bfloat16 [8192, 8192], P('batch', 'weight'), may hold values from -0.0625 to 0.0625
- key_weight: bfloat16 [8192, 1024], P('batch'), may hold values from -0.0625 to 0.0625
- value_weight: bfloat16 [8192, 1024], P('batch'), may hold values from -0.0625 to 0.0625
Outputs:
- attended: bfloat16 [16384, 8192], P('batch', 'weight')
Inputs may be any that keep to these rules, and one draw needn't show every extreme that they name: `segment_ids`: segment ids never fall along the tokens; each id covers 1 to 64 consecutive tokens, one of them exactly 64.
All inputs are finite; a program needn't handle non-finite values.
Results may differ from a plain program's by a relative error of at most 0.0079.
Values may be sent and summed in bfloat16 or wider, within the bound.
No kernel may reach another device: no remote copies, remote signals or barrier semaphores. Data moves between devices by JAX's collectives and lax.ppermute only.
A program may use at most 64 MiB of HBM per device.

v0:
```python
import math
import jax
import jax.numpy as jnp
from jax import lax
from jax.sharding import PartitionSpec as P

HEADS = 64
KV_HEADS = 8
HEAD_DIM = 128
ROPE_BASE = 500000.0
EPSILON = 1e-05


def positions_in_segment(seg_ids):
    places = jnp.arange(seg_ids.shape[0], dtype=jnp.int32)
    earlier = jnp.concatenate([seg_ids[:1] - 1, seg_ids[:-1]])
    starts = jnp.where(seg_ids != earlier, places, 0)
    leading = lax.cummax(starts, axis=0)
    return places - leading


def rotate(vectors, positions):
    half_dim = vectors.shape[-1] // 2
    ratios = jnp.arange(half_dim, dtype=jnp.float32) * (2.0 / vectors.shape[-1])
    frequency = jnp.exp(-math.log(ROPE_BASE) * ratios)
    angles = positions.astype(jnp.float32)[:, None] * frequency[None, :]
    cosine = jnp.cos(angles)[:, None, :]
    sine_part = jnp.sin(angles)[:, None, :]
    front_half = vectors[..., :half_dim]
    back_half = vectors[..., half_dim:]
    return jnp.concatenate(
        [front_half * cosine - back_half * sine_part, back_half * cosine + front_half * sine_part],
        axis=-1,
    )


def attend(grouped, rotated_keys, value_rows, seg_ids):
    scores = jnp.einsum(
        "ingd,jnd->ngij", grouped, rotated_keys, preferred_element_type=jnp.float32
    ) * grouped.shape[-1] ** (-0.5)
    places = jnp.arange(seg_ids.shape[0], dtype=jnp.int32)
    allowed = (seg_ids[:, None] == seg_ids[None, :]) & (places[None, :] <= places[:, None])
    weights = jnp.where(allowed, jnp.exp(scores), 0.0)
    probabilities = (weights / jnp.sum(weights, axis=-1, keepdims=True)).astype(jnp.bfloat16)
    mixed = jnp.einsum(
        "ngij,jnd->ingd", probabilities, value_rows, preferred_element_type=jnp.float32
    )
    return mixed.astype(jnp.bfloat16)


def per_device(tokens, segment_ids, norm_gain, query_weight, key_weight, value_weight):
    head_dim = HEAD_DIM
    query_cols = query_weight.shape[1]
    heads_dev = query_cols // head_dim
    group_size = HEADS // KV_HEADS
    local_kv = max(1, heads_dev // group_size)
    first_kv = lax.axis_index("weight") * heads_dev // group_size
    key_width = local_kv * head_dim
    key_block = lax.dynamic_slice_in_dim(key_weight, first_kv * head_dim, key_width, 1)
    value_block = lax.dynamic_slice_in_dim(value_weight, first_kv * head_dim, key_width, 1)
    values = tokens.astype(jnp.float32)
    inverse_rms = lax.rsqrt(jnp.mean(values * values, axis=1, keepdims=True) + EPSILON)
    normed = (values * inverse_rms * norm_gain[None, :]).astype(jnp.bfloat16)
    local_weights = jnp.concatenate([query_weight, key_block, value_block], axis=1)
    full_weights = lax.all_gather(local_weights, "batch", axis=0, tiled=True)
    projected = jnp.dot(
        lax.all_gather(normed, "weight", axis=0, tiled=True),
        full_weights,
        preferred_element_type=jnp.float32,
    )
    query_part = projected[:, :query_cols]
    key_rows = projected[:, query_cols : query_cols + key_width].astype(jnp.bfloat16)
    value_rows = projected[:, query_cols + key_width :].astype(jnp.bfloat16)
    pack_rows = projected.shape[0]
    positions = positions_in_segment(segment_ids)
    queries = rotate(query_part.reshape(pack_rows, heads_dev, head_dim), positions).astype(
        jnp.bfloat16
    )
    rotated_keys = rotate(
        key_rows.astype(jnp.float32).reshape(pack_rows, local_kv, head_dim), positions
    ).astype(jnp.bfloat16)
    grouped = queries.reshape(pack_rows, local_kv, heads_dev // local_kv, head_dim)
    attended = attend(
        grouped, rotated_keys, value_rows.reshape(pack_rows, local_kv, head_dim), segment_ids
    )
    return attended.reshape(pack_rows, query_cols)


def solution(mesh):
    placed = (
        P(("batch", "weight"), None),
        P("batch"),
        P(),
        P("batch", "weight"),
        P("batch", None),
        P("batch", None),
    )
    return jax.shard_map(
        per_device, mesh=mesh, in_specs=placed, out_specs=P("batch", "weight"), check_vma=False
    )
```

profile of v0, /device:TPU:1, one launch (start us, length us, event | category | flops | bytes accessed | tf_op | source)
XLA Modules:
  0.0 284.9 jit_solution(18422892970738844618)
XLA Ops:
  6.5 1.2 fusion.7
  7.8 2.0 fusion.9
  9.9 0.9 constant_dynamic-slice_fusion
  10.8 1.7 pad_maximum_fusion
  12.6 1.3 slice.39
  14.5 0.8 select_bitcast_fusion
  15.3 0.3 reduce-window.9
  15.7 0.1 slice.41
  15.8 0.1 slice_reduce_fusion
  15.9 0.1 fusion.28
  16.0 1.0 fusion.10
  16.9 1.0 multiply_cosine_fusion
  17.9 55.4 %all-gather.3.cloned.1.call-done = bf16[512,8192]{1,0:T(8,128)(2,1)} async-done(((bf16[32,8192]{1,0:T(8,128)(2,1)}), bf16[512,8192]{1,0:T(8,128)(2,1)}) %all-gather.3.cloned.1.call-update) | async-done | bytes 8388624 | tf_op jit(solution)/shard_map/all_gather | solution.py:67
  73.4 183.1 %all-gather.5.cloned.1.call-done = bf16[8192,768]{1,0:T(8,128)(2,1)} async-done(((bf16[256,768]{1,0:T(8,128)(2,1)}), bf16[8192,768]{1,0:T(8,128)(2,1)}) %all-gather.5.cloned.1.call-update) | async-done | bytes 12582928 | tf_op jit(solution)/shard_map/all_gather | solution.py:65
  256.4 13.4 %fusion.33 = (bf16[512,768]{1,0:T(8,128)(2,1)}, f32[512,768]{1,0:T(8,128)S(1)}) fusion(bf16[512,8192]{1,0:T(8,128)(2,1)} %all-gather.3.cloned.1.call-done, bf16[8192,768]{1,0:T(8,128)(2,1)} %all-gather.5.cloned.1.call-done), kind=kOutput, calls=%fused_computation.54 | convolution fusion | flops 6442844160 | bytes 23330816 | tf_op jit(solution)/shard_map/dot_general | solution.py:66
  269.9 0.1 slice.51
  270.0 0.4 reshape.192
  270.4 0.6 fusion.32
  271.0 0.9 fusion.23
  271.9 1.2 fusion.27
  273.1 0.3 subtract_convert_fusion
  273.4 1.5 fusion
  274.9 2.2 fusion.4
  277.1 1.0 copy.16
  (7 shorter events, 0.1 us)
Async XLA Ops:
  6.5 66.8 %all-gather.3.cloned.1.call-start = ((), (), s32[]{:S(2)}) async-start(), calls=%async_computation | async-start | bytes 8912896 | tf_op jit(solution)/shard_map/all_gather | solution.py:67
  9.9 246.6 %all-gather.5.cloned.1.call-start = ((), (), s32[]{:S(2)}) async-start(), calls=%async_computation.1 | async-start | bytes 12976128 | tf_op jit(solution)/shard_map/all_gather | solution.py:65
Sparse Core Ops, SparseCore 0:
  10.0 63.3 all-gather.2
  76.5 179.8 all-gather.4
where the time goes:
time: 285 us
  waiting for transfers between devices  239 us (84%)
  matrix products  17.1 us (6%)
  between operations  14.2 us (5%)
  other arithmetic  10.7 us (4%)
  local copies, waits for them, and re-layouts  4.42 us (2%)
    all_gather x1, waiting for transfers between devices, per_device(): full_weights = lax.all_gather(local_weights, 'batch', axis=0, tiled=True)  183 us
    all_gather x1, waiting for transfers between devices, per_device(): lax.all_gather(normed, 'weight', axis=0, tiled=True)  55.4 us
    dot_general x1, matrix products, per_device(): jnp.dot(lax.all_gather(normed, 'weight', axis=0, tiled=True), full_weight...  13.4 us
  transfers between devices with their start and end apart: 2, of which 2 were waited for; matrix products, arithmetic and copies ran while one was open for 3% of the time, Pallas kernels for 0%

commit v1 on v0

--- a/solution.py
+++ b/solution.py
@@ -62,7 +62,8 @@
     inverse_rms = lax.rsqrt(jnp.mean(values * values, axis=1, keepdims=True) + EPSILON)
     normed = (values * inverse_rms * norm_gain[None, :]).astype(jnp.bfloat16)
     local_weights = jnp.concatenate([query_weight, key_block, value_block], axis=1)
-    full_weights = lax.all_gather(local_weights, "batch", axis=0, tiled=True)
+    outgoing = jnp.stack([local_weights] * lax.axis_size("batch"))
+    full_weights = jnp.concatenate(lax.all_to_all(outgoing, "batch", 0, 0), axis=0)
     projected = jnp.dot(
         lax.all_gather(normed, "weight", axis=0, tiled=True),
         full_weights,

time: 285 us -> 509 us (1.79)
  the two profiles are of different devices: /device:TPU:1 before, /device:TPU:360 now
where the time goes in v1:
time: 509 us
  waiting for transfers between devices  450 us (88%)
  matrix products  17.2 us (3%)
  between operations  14.1 us (3%)
  starting transfers between devices  11.5 us (2%)
  local copies, waits for them, and re-layouts  9.63 us (2%)
  other arithmetic  6.33 us (1%)
    all_to_all x1, waiting for transfers between devices, per_device(): lax.all_to_all(outgoing, 'batch', 0, 0)  266 us
    all_gather x1, waiting for transfers between devices, per_device(): lax.all_gather(normed, 'weight', axis=0, tiled=True)  184 us
    dot_general x1, matrix products, per_device(): jnp.dot(lax.all_gather(normed, 'weight', axis=0, tiled=True), full_weight...  13.5 us
    all_to_all x1, starting transfers between devices, per_device(): lax.all_to_all(outgoing, 'batch', 0, 0)  11.5 us
  transfers between devices with their start and end apart: 2, of which 2 were waited for; matrix products, arithmetic and copies ran while one was open for 1% of the time, Pallas kernels for 0%

profile of v1, /device:TPU:360, one launch (start us, length us, event | category | flops | bytes accessed | tf_op | source)
XLA Modules:
  0.0 508.7 jit_solution(6105842424092136823)
XLA Ops:
  6.5 0.9 constant_dynamic-slice_fusion
  7.4 1.0 pad_maximum_fusion
  8.4 5.9 %stack.2 = bf16[32,256,768]{2,1,0:T(8,128)(2,1)} broadcast(bf16[256,768]{1,0:T(8,128)(2,1)S(1)} %pad_maximum_fusion), dimensions={1,2} | broadcast | bytes 12976128 | tf_op jit(solution)/shard_map/stack | solution.py:65
  14.3 11.5 %all-to-all-start = ((bf16[32,256,768]{2,1,0:T(8,128)(2,1)}), bf16[32,256,768]{2,1,0:T(8,128)(2,1)}, u32[]{:S(2)}, u32[]{:S(2)}) async-start(bf16[32,256,768]{2,1,0:T(8,128)(2,1)} %stack.2), calls=%async_computation | async-start | bytes 25165824 | tf_op jit(solution)/shard_map/all_to_all | solution.py:66
  25.9 0.2 fusion.7
  26.1 1.0 fusion.9
  27.1 0.5 slice.39
  28.3 0.1 select_bitcast_fusion
  28.4 0.3 reduce-window.9
  28.8 0.1 slice_reduce_fusion
  29.0 0.2 fusion.10
  29.2 1.0 multiply_cosine_fusion
  30.2 184.1 %all-gather.2.cloned.1.call-done = bf16[512,8192]{1,0:T(8,128)(2,1)} async-done(((bf16[32,8192]{1,0:T(8,128)(2,1)}), bf16[512,8192]{1,0:T(8,128)(2,1)}) %all-gather.2.cloned.1.call-update) | async-done | bytes 8388624 | tf_op jit(solution)/shard_map/all_gather | solution.py:68
  214.3 265.9 %all-to-all-done = bf16[32,256,768]{2,1,0:T(8,128)(2,1)} async-done(((bf16[32,256,768]{2,1,0:T(8,128)(2,1)}), bf16[32,256,768]{2,1,0:T(8,128)(2,1)}, u32[]{:S(2)}, u32[]{:S(2)}) %all-to-all-start) | async-done | bytes 12582944 | tf_op jit(solution)/shard_map/all_to_all | solution.py:66
  480.1 13.5 %fusion.33 = (bf16[512,768]{1,0:T(8,128)(2,1)}, f32[512,768]{1,0:T(8,128)S(1)}) fusion(bf16[512,8192]{1,0:T(8,128)(2,1)} %all-gather.2.cloned.1.call-done, bf16[8192,768]{1,0:T(8,128)(2,1)} %bitcast), kind=kOutput, calls=%fused_computation.54 | convolution fusion | flops 6442844160 | bytes 23330816 | tf_op jit(solution)/shard_map/dot_general | solution.py:67
  493.6 0.1 slice.51
  493.8 0.4 reshape.198
  494.1 0.6 fusion.32
  494.7 0.9 fusion.23
  495.7 1.2 fusion.27
  496.9 0.3 subtract_convert_fusion
  497.2 1.5 fusion
  498.6 2.2 fusion.4
  500.9 1.0 copy.16
  (13 shorter events, 0.3 us)
Async XLA Ops:
  14.3 11.6 %copy-start = (bf16[32,8192]{1,0:T(8,128)(2,1)S(1)}, bf16[32,8192]{1,0:T(8,128)(2,1)}, u32[]{:S(2)}) copy-start(bf16[32,8192]{1,0:T(8,128)(2,1)} %param.6) | copy-start | bytes 1572868
  14.3 11.8 %copy-start.2 = (f32[8192]{0:T(1024)S(1)}, f32[8192]{0:T(1024)}, u32[]{:S(2)}) copy-start(f32[8192]{0:T(1024)} %param.8) | copy-start | bytes 98308
  14.3 12.8 %copy-start.1 = (s32[512]{0:T(512)S(1)}, s32[512]{0:T(512)}, u32[]{:S(2)}) copy-start(s32[512]{0:T(512)} %param.7) | copy-start | bytes 6148
  14.3 465.8 %all-to-all-start = ((bf16[32,256,768]{2,1,0:T(8,128)(2,1)}), bf16[32,256,768]{2,1,0:T(8,128)(2,1)}, u32[]{:S(2)}, u32[]{:S(2)}) async-start(bf16[32,256,768]{2,1,0:T(8,128)(2,1)} %stack.2), calls=%async_computation | async-start | bytes 25165824 | tf_op jit(solution)/shard_map/all_to_all | solution.py:66
  25.8 188.5 %all-gather.2.cloned.1.call-start = ((), (), s32[]{:S(2)}) async-start(), calls=%async_computation.1 | async-start | bytes 8912896 | tf_op jit(solution)/shard_map/all_gather | solution.py:68
Sparse Core Ops, SparseCore 0:
  28.8 185.4 all-gather.1
